TPU v7x, 512 devices: a whole 4x4x16 slice. The times are simulated.
512 devices in a mesh: fine: 128 (over y, z, core), tele: 4 (over x).
Axes of the slice: x: 4, y: 4, z: 16, core: 2. Of those that a mesh axis runs over, the one named last changes fastest.
Arguments:
- right_side: float32 [8192, 320], P(('fine', 'tele')), may hold values from -6 to 6
- fine_inverse: bfloat16 [8192, 320, 320], P(('fine', 'tele')), may hold values from -0.08 to 0.45
- fine_links: int32 [8192, 6], P(('fine', 'tele')), may hold values from -1 to 8191, as said below
- fine_faces: int32 [8192, 6], P(('fine', 'tele')), may hold values from 0 to 23
- coarse_inverse: bfloat16 [1024, 320, 320], P(('fine', 'tele')), may hold values from -0.04 to 0.21
- coarse_links: int32 [1024, 6], P(('fine', 'tele')), may hold values from -1 to 1023, as said below
- coarse_faces: int32 [1024, 6], P(('fine', 'tele')), may hold values from 0 to 23
- face_operators: bfloat16 [24, 80, 80], replicated, may hold values from -1.25 to 1.25
- agglomerate: int32 [8192], P(('fine', 'tele')), may hold values from 0 to 1023, as said below
Outputs:
- solution: float32 [8192, 320], P(('fine', 'tele'))
Inputs may be any that keep to these rules, and one draw needn't show every extreme that they name: `fine_links`: any entry other than -1 is an element held by the same device as the element, or by the device just before or after it in the order of fine+tele, cyclically. `coarse_links`: coarse elements form blocks of 8 consecutive ones; any entry other than -1 lies in the element's own block or in the block just before or after it, cyclically. `agglomerate`: fine element i maps into block i // 64 of 8 consecutive coarse elements; every coarse element collects exactly 8 fine elements.
All inputs are finite; a program needn't handle non-finite values.
Results may differ from a plain program's by a relative error of at most 0.02.
Values may be sent and summed in bfloat16 or wider, within the bound.
No kernel may reach another device: no remote copies, remote signals or barrier semaphores. Data moves between devices by JAX's collectives and lax.ppermute only.
A program may use at most 64 MiB of HBM per device.

v0:
```python
import jax
import jax.numpy as jnp
from jax import lax
from jax.sharding import PartitionSpec as P

FIELDS = 5
NODES = 4
SWEEPS = 3
CYCLES = 2
OPPOSITE = (1, 0, 3, 2, 5, 4)


def passed_along(block, axis, distance):
    devices = range(lax.axis_size(axis))
    route = [((i - distance) % len(devices), i) for i in devices]
    return lax.ppermute(block, axis, route)


def face_table():
    face_size = NODES * NODES
    column = jnp.arange(6 * FIELDS * face_size, dtype=jnp.int32)
    face_index = column // (FIELDS * face_size)
    within = column % (FIELDS * face_size)
    field_index = within // face_size
    first = within // NODES % NODES
    second = within % NODES
    far_node = NODES - 1
    side = jnp.where(face_index % 2 == 0, 0, far_node)
    node_a = jnp.where(face_index < 2, side, first)
    node_b = jnp.where(face_index < 2, first, jnp.where(face_index < 4, side, second))
    node_c = jnp.where(face_index < 4, second, side)
    target = ((field_index * NODES + node_a) * NODES + node_b) * NODES + node_c
    dof_index = jnp.arange(FIELDS * NODES * NODES * NODES, dtype=jnp.int32)
    return (dof_index[:, None] == target[None, :]).astype(jnp.float32)


def take_traces(field_state, table):
    row_count = field_state.shape[0]
    picked = jnp.dot(
        field_state, table, precision=lax.Precision.HIGHEST, preferred_element_type=jnp.float32
    )
    return picked.astype(jnp.bfloat16).reshape(row_count, 6, -1)


def lift_faces(coupled, table):
    return lax.dot_general(
        coupled,
        table,
        (((1,), (1,)), ((), ())),
        precision=lax.Precision.HIGHEST,
        preferred_element_type=jnp.float32,
    )


def neighbour_rows(preceding, own_traces, following, links, position, row_count, devices):
    trace_pool = jnp.concatenate([preceding, own_traces, following], axis=0).reshape(
        -1, own_traces.shape[2]
    )
    clamped = jnp.maximum(links, 0)
    relative = (clamped // row_count - position + 1) % devices
    opposite = jnp.array(OPPOSITE, jnp.int32)
    row_index = (relative * row_count + clamped % row_count) * 6 + opposite[None, :]
    face_rows = jnp.take(trace_pool, row_index.reshape(-1), axis=0).reshape(links.shape[0], 6, -1)
    return jnp.where((links >= 0)[:, :, None], face_rows, jnp.zeros_like(face_rows))


def face_apply(face_operators, face_rows, faces, table):
    flat_rows = face_rows.reshape(-1, face_rows.shape[2])
    face_kinds = faces.reshape(-1)
    products = jnp.einsum(
        "rk,qjk->rqj", flat_rows, face_operators, preferred_element_type=jnp.float32
    )
    picked = face_kinds[:, None] == jnp.arange(face_operators.shape[0], dtype=jnp.int32)[None, :]
    result = jnp.sum(jnp.where(picked[:, :, None], products, 0.0), axis=1)
    return lift_faces(result.reshape(face_rows.shape[0], -1), table)


def fine_coupling(field_state, face_operators, links, faces, position, devices, table):
    own_traces = take_traces(field_state, table)
    preceding = passed_along(own_traces, ("fine", "tele"), 1)
    following = passed_along(own_traces, ("fine", "tele"), -1)
    face_rows = neighbour_rows(
        preceding, own_traces, following, links, position, field_state.shape[0], devices
    )
    return face_apply(face_operators, face_rows, faces, table)


def coarse_coupling(column_traces, face_operators, links, faces, position, devices, table):
    preceding = passed_along(column_traces, "fine", 1)
    following = passed_along(column_traces, "fine", -1)
    face_rows = neighbour_rows(
        preceding, column_traces, following, links, position, column_traces.shape[0], devices
    )
    return face_apply(face_operators, face_rows, faces, table)


def apply_inverse(inverse, lowered):
    return jnp.einsum("nij,nj->ni", inverse, lowered, preferred_element_type=jnp.float32)


def shards(
    right_side,
    fine_inverse,
    fine_links,
    fine_faces,
    coarse_inverse,
    coarse_links,
    coarse_faces,
    face_operators,
    agglomerate,
):
    table = face_table()
    tele_size = lax.axis_size("tele")
    fine_position = lax.axis_index("fine") * tele_size + lax.axis_index("tele")
    fine_devices = lax.axis_size("fine") * tele_size
    column_position = lax.axis_index("fine")
    columns = lax.axis_size("fine")
    column_rows = coarse_inverse.shape[0] * tele_size
    local_target = agglomerate % column_rows
    member = (local_target[:, None] == jnp.arange(column_rows, dtype=jnp.int32)[None, :]).astype(
        jnp.float32
    )
    block_inverse = lax.all_gather(coarse_inverse, "tele", axis=0, tiled=True)
    index_lists = lax.all_gather(
        jnp.concatenate([coarse_links, coarse_faces], axis=1), "tele", axis=0, tiled=True
    )
    block_links = index_lists[:, :6]
    block_faces = index_lists[:, 6:]
    solution = jnp.zeros(right_side.shape, jnp.float32)
    for cycle_index in range(CYCLES):
        for sweep_index in range(SWEEPS):
            if cycle_index == 0 and sweep_index == 0:
                coupled = jnp.zeros(right_side.shape, jnp.float32)
            else:
                coupled = fine_coupling(
                    solution,
                    face_operators,
                    fine_links,
                    fine_faces,
                    fine_position,
                    fine_devices,
                    table,
                )
            lowered = (right_side - coupled).astype(jnp.bfloat16)
            solution = apply_inverse(fine_inverse, lowered)
        residual = lowered.astype(jnp.float32) - fine_coupling(
            solution, face_operators, fine_links, fine_faces, fine_position, fine_devices, table
        )
        partial_sum = jnp.dot(
            member.T, residual, precision=lax.Precision.HIGHEST, preferred_element_type=jnp.float32
        )
        restricted = lax.psum(partial_sum, "tele")
        coarse_state = apply_inverse(block_inverse, restricted.astype(jnp.bfloat16))
        for sweep_index in range(SWEEPS - 1):
            coupled_coarse = coarse_coupling(
                take_traces(coarse_state, table),
                face_operators,
                block_links,
                block_faces,
                column_position,
                columns,
                table,
            )
            coarse_state = apply_inverse(
                block_inverse, (restricted - coupled_coarse).astype(jnp.bfloat16)
            )
        solution = solution + jnp.take(coarse_state, local_target, axis=0)
    return solution


def solution(mesh):
    return jax.shard_map(
        shards,
        mesh=mesh,
        in_specs=(
            P(("fine", "tele"), None),
            P(("fine", "tele"), None, None),
            P(("fine", "tele"), None),
            P(("fine", "tele"), None),
            P(("fine", "tele"), None, None),
            P(("fine", "tele"), None),
            P(("fine", "tele"), None),
            P(),
            P(("fine", "tele")),
        ),
        out_specs=P(("fine", "tele"), None),
        check_vma=False,
    )
```

profile of v0, /device:TPU:2, one launch (start us, length us, event | category | flops | bytes accessed | tf_op | source)
XLA Modules:
  0.0 242.5 jit_solution(18185007734287332940)
XLA Ops:
  7.5 3.3 %fusion.76 = f32[16,1,320]{2,1,0:T(1,128)S(1)} fusion(bf16[16,320,320]{2,1,0:T(8,128)(2,1)} %param.27, bf16[16,320,1]{1,0,2:T(8,128)(2,1)S(1)} %convert_bitcast_fusion), kind=kOutput, calls=%fused_computation.136 | convolution fusion | flops 3276800 | bytes 3307520 | tf_op jit(solution)/shard_map/nij,nj->ni/dot_general | solution.py:98
  11.3 7.8 %collective-permute-start.1 = (bf16[16,6,80]{2,1,0:T(8,128)(2,1)S(1)}, bf16[16,6,80]{2,1,0:T(8,128)(2,1)S(1)}, u32[]{:S(2)}, u32[]{:S(2)}) collective-permute-start(bf16[16,6,80]{2,1,0:T(8,128)(2,1)S(1)} %reshape.333), channel_id=1, source_target_pairs={{1,0},{2,1},{3,2},{4,3},{5,4},{6,5},{7,6},{8,7},{9,8},{10,9},{11,1... | collective-permute-start | bytes 46088 | tf_op jit(solution)/shard_map/ppermute | solution.py:16
  21.2 15.2 %all-gather = s32[4,2,12]{2,1,0:T(2,128)S(1)} all-gather(s32[1,2,12]{2,1,0:T(2,128)S(1)} %add_bitcast_fusion), channel_id=1, replica_groups=mesh['fine'=128,'tele'=4] {'tele'}, dimensions={0}, use_global_device_ids=true | all-gather | bytes 480 | tf_op jit(solution)/shard_map/all_gather | solution.py:124
  39.0 3.5 %fusion.73 = f32[16,1,320]{2,1,0:T(1,128)S(1)} fusion(bf16[16,320,320]{2,1,0:T(8,128)(2,1)} %param.27, bf16[16,320,1]{1,0,2:T(8,128)(2,1)S(1)} %fusion.18), kind=kOutput, calls=%fused_computation.133 | convolution fusion | flops 3276800 | bytes 3307520 | tf_op jit(solution)/shard_map/nij,nj->ni/dot_general | solution.py:98
  43.0 2.6 %collective-permute-start.3 = (bf16[16,6,80]{2,1,0:T(8,128)(2,1)S(1)}, bf16[16,6,80]{2,1,0:T(8,128)(2,1)S(1)}, u32[]{:S(2)}, u32[]{:S(2)}) collective-permute-start(bf16[16,6,80]{2,1,0:T(8,128)(2,1)S(1)} %reshape.337), channel_id=1, source_target_pairs={{1,0},{2,1},{3,2},{4,3},{5,4},{6,5},{7,6},{8,7},{9,8},{10,9},{11,1... | collective-permute-start | bytes 46088 | tf_op jit(solution)/shard_map/ppermute | solution.py:16
  45.5 3.3 %collective-permute-start.2 = (bf16[16,6,80]{2,1,0:T(8,128)(2,1)S(1)}, bf16[16,6,80]{2,1,0:T(8,128)(2,1)S(1)}, u32[]{:S(2)}, u32[]{:S(2)}) collective-permute-start(bf16[16,6,80]{2,1,0:T(8,128)(2,1)S(1)} %reshape.337), channel_id=1, source_target_pairs={{511,0},{0,1},{1,2},{2,3},{3,4},{4,5},{5,6},{6,7},{7,8},{8,9},{9,1... | collective-permute-start | bytes 46088 | tf_op jit(solution)/shard_map/ppermute | solution.py:16
  49.5 4.9 %collective-permute-done.2 = bf16[16,6,80]{2,1,0:T(8,128)(2,1)S(1)} collective-permute-done((bf16[16,6,80]{2,1,0:T(8,128)(2,1)S(1)}, bf16[16,6,80]{2,1,0:T(8,128)(2,1)S(1)}, u32[]{:S(2)}, u32[]{:S(2)}) %collective-permute-start.2) | collective-permute-done | bytes 15392 | tf_op jit(solution)/shard_map/ppermute | solution.py:16
  56.0 3.3 %fusion.70 = f32[16,1,320]{2,1,0:T(1,128)S(1)} fusion(bf16[16,320,320]{2,1,0:T(8,128)(2,1)} %param.27, bf16[16,320,1]{1,0,2:T(8,128)(2,1)S(1)} %bitcast.138), kind=kOutput, calls=%fused_computation.130 | convolution fusion | flops 3276800 | bytes 3307520 | tf_op jit(solution)/shard_map/nij,nj->ni/dot_general | solution.py:98
  59.8 8.2 %collective-permute-start.5 = (bf16[16,6,80]{2,1,0:T(8,128)(2,1)S(1)}, bf16[16,6,80]{2,1,0:T(8,128)(2,1)S(1)}, u32[]{:S(2)}, u32[]{:S(2)}) collective-permute-start(bf16[16,6,80]{2,1,0:T(8,128)(2,1)S(1)} %reshape.341), channel_id=1, source_target_pairs={{1,0},{2,1},{3,2},{4,3},{5,4},{6,5},{7,6},{8,7},{9,8},{10,9},{11,1... | collective-permute-start | bytes 46088 | tf_op jit(solution)/shard_map/ppermute | solution.py:16
  70.0 3.9 %collective-permute-done.4 = bf16[16,6,80]{2,1,0:T(8,128)(2,1)S(1)} collective-permute-done((bf16[16,6,80]{2,1,0:T(8,128)(2,1)S(1)}, bf16[16,6,80]{2,1,0:T(8,128)(2,1)S(1)}, u32[]{:S(2)}, u32[]{:S(2)}) %collective-permute-start.4) | collective-permute-done | bytes 15392 | tf_op jit(solution)/shard_map/ppermute | solution.py:16
  75.8 17.8 %psum.14 = f32[8,320]{1,0:T(8,128)S(1)} all-reduce(f32[8,320]{1,0:T(8,128)S(1)} %fusion.145), channel_id=1, replica_groups=mesh['fine'=128,'tele'=4] {'tele'}, use_global_device_ids=true, to_apply=%region_3.5 | all-reduce | flops 2560 | bytes 20480 | tf_op jit(solution)/shard_map/psum | solution.py:152
  98.2 2.4 collective-permute-start.6
  100.8 5.9 %collective-permute-done.6 = bf16[8,6,80]{2,1,0:T(8,128)(2,1)S(1)} collective-permute-done((bf16[8,6,80]{2,1,0:T(8,128)(2,1)S(1)}, bf16[8,6,80]{2,1,0:T(8,128)(2,1)S(1)}, u32[]{:S(2)}, u32[]{:S(2)}) %collective-permute-start.6) | collective-permute-done | bytes 7712 | tf_op jit(solution)/shard_map/ppermute | solution.py:16
  112.8 2.4 collective-permute-start.8
  115.3 5.9 %collective-permute-done.8 = bf16[8,6,80]{2,1,0:T(8,128)(2,1)S(1)} collective-permute-done((bf16[8,6,80]{2,1,0:T(8,128)(2,1)S(1)}, bf16[8,6,80]{2,1,0:T(8,128)(2,1)S(1)}, u32[]{:S(2)}, u32[]{:S(2)}) %collective-permute-start.8) | collective-permute-done | bytes 7712 | tf_op jit(solution)/shard_map/ppermute | solution.py:16
  124.5 3.3 %collective-permute-start.11 = (bf16[16,6,80]{2,1,0:T(8,128)(2,1)S(1)}, bf16[16,6,80]{2,1,0:T(8,128)(2,1)S(1)}, u32[]{:S(2)}, u32[]{:S(2)}) collective-permute-start(bf16[16,6,80]{2,1,0:T(8,128)(2,1)S(1)} %reshape.353), channel_id=1, source_target_pairs={{1,0},{2,1},{3,2},{4,3},{5,4},{6,5},{7,6},{8,7},{9,8},{10,9},{11,1... | collective-permute-start | bytes 46088 | tf_op jit(solution)/shard_map/ppermute | solution.py:16
  127.9 2.5 %collective-permute-start.10 = (bf16[16,6,80]{2,1,0:T(8,128)(2,1)S(1)}, bf16[16,6,80]{2,1,0:T(8,128)(2,1)S(1)}, u32[]{:S(2)}, u32[]{:S(2)}) collective-permute-start(bf16[16,6,80]{2,1,0:T(8,128)(2,1)S(1)} %reshape.353), channel_id=1, source_target_pairs={{511,0},{0,1},{1,2},{2,3},{3,4},{4,5},{5,6},{6,7},{7,8},{8,9},{9,1... | collective-permute-start | bytes 46088 | tf_op jit(solution)/shard_map/ppermute | solution.py:16
  130.4 3.3 %collective-permute-done.10 = bf16[16,6,80]{2,1,0:T(8,128)(2,1)S(1)} collective-permute-done((bf16[16,6,80]{2,1,0:T(8,128)(2,1)S(1)}, bf16[16,6,80]{2,1,0:T(8,128)(2,1)S(1)}, u32[]{:S(2)}, u32[]{:S(2)}) %collective-permute-start.10) | collective-permute-done | bytes 15392 | tf_op jit(solution)/shard_map/ppermute | solution.py:16
  135.4 3.3 %fusion.68 = f32[16,1,320]{2,1,0:T(1,128)S(1)} fusion(bf16[16,320,320]{2,1,0:T(8,128)(2,1)} %param.27, bf16[16,320,1]{1,0,2:T(8,128)(2,1)S(1)} %fusion.17), kind=kOutput, calls=%fused_computation.128 | convolution fusion | flops 3276800 | bytes 3307520 | tf_op jit(solution)/shard_map/nij,nj->ni/dot_general | solution.py:98
  139.1 6.9 %collective-permute-start.13 = (bf16[16,6,80]{2,1,0:T(8,128)(2,1)S(1)}, bf16[16,6,80]{2,1,0:T(8,128)(2,1)S(1)}, u32[]{:S(2)}, u32[]{:S(2)}) collective-permute-start(bf16[16,6,80]{2,1,0:T(8,128)(2,1)S(1)} %reshape.357), channel_id=1, source_target_pairs={{1,0},{2,1},{3,2},{4,3},{5,4},{6,5},{7,6},{8,7},{9,8},{10,9},{11,1... | collective-permute-start | bytes 46088 | tf_op jit(solution)/shard_map/ppermute | solution.py:16
  148.2 3.7 %collective-permute-done.12 = bf16[16,6,80]{2,1,0:T(8,128)(2,1)S(1)} collective-permute-done((bf16[16,6,80]{2,1,0:T(8,128)(2,1)S(1)}, bf16[16,6,80]{2,1,0:T(8,128)(2,1)S(1)}, u32[]{:S(2)}, u32[]{:S(2)}) %collective-permute-start.12) | collective-permute-done | bytes 15392 | tf_op jit(solution)/shard_map/ppermute | solution.py:16
  153.5 3.3 %fusion.65 = f32[16,1,320]{2,1,0:T(1,128)S(1)} fusion(bf16[16,320,320]{2,1,0:T(8,128)(2,1)} %param.27, bf16[16,320,1]{1,0,2:T(8,128)(2,1)S(1)} %fusion.16), kind=kOutput, calls=%fused_computation.125 | convolution fusion | flops 3276800 | bytes 3307520 | tf_op jit(solution)/shard_map/nij,nj->ni/dot_general | solution.py:98
  157.3 6.8 %collective-permute-start.15 = (bf16[16,6,80]{2,1,0:T(8,128)(2,1)S(1)}, bf16[16,6,80]{2,1,0:T(8,128)(2,1)S(1)}, u32[]{:S(2)}, u32[]{:S(2)}) collective-permute-start(bf16[16,6,80]{2,1,0:T(8,128)(2,1)S(1)} %reshape.361), channel_id=1, source_target_pairs={{1,0},{2,1},{3,2},{4,3},{5,4},{6,5},{7,6},{8,7},{9,8},{10,9},{11,1... | collective-permute-start | bytes 46088 | tf_op jit(solution)/shard_map/ppermute | solution.py:16
  166.0 3.9 %collective-permute-done.14 = bf16[16,6,80]{2,1,0:T(8,128)(2,1)S(1)} collective-permute-done((bf16[16,6,80]{2,1,0:T(8,128)(2,1)S(1)}, bf16[16,6,80]{2,1,0:T(8,128)(2,1)S(1)}, u32[]{:S(2)}, u32[]{:S(2)}) %collective-permute-start.14) | collective-permute-done | bytes 15392 | tf_op jit(solution)/shard_map/ppermute | solution.py:16
  171.6 3.3 %fusion.62 = f32[16,1,320]{2,1,0:T(1,128)S(1)} fusion(bf16[16,320,320]{2,1,0:T(8,128)(2,1)} %param.27, bf16[16,320,1]{1,0,2:T(8,128)(2,1)S(1)} %bitcast.137), kind=kOutput, calls=%fused_computation.122 | convolution fusion | flops 3276800 | bytes 3307520 | tf_op jit(solution)/shard_map/nij,nj->ni/dot_general | solution.py:98
  175.3 6.8 %collective-permute-start.17 = (bf16[16,6,80]{2,1,0:T(8,128)(2,1)S(1)}, bf16[16,6,80]{2,1,0:T(8,128)(2,1)S(1)}, u32[]{:S(2)}, u32[]{:S(2)}) collective-permute-start(bf16[16,6,80]{2,1,0:T(8,128)(2,1)S(1)} %reshape.365), channel_id=1, source_target_pairs={{1,0},{2,1},{3,2},{4,3},{5,4},{6,5},{7,6},{8,7},{9,8},{10,9},{11,1... | collective-permute-start | bytes 46088 | tf_op jit(solution)/shard_map/ppermute | solution.py:16
  184.1 3.9 %collective-permute-done.16 = bf16[16,6,80]{2,1,0:T(8,128)(2,1)S(1)} collective-permute-done((bf16[16,6,80]{2,1,0:T(8,128)(2,1)S(1)}, bf16[16,6,80]{2,1,0:T(8,128)(2,1)S(1)}, u32[]{:S(2)}, u32[]{:S(2)}) %collective-permute-start.16) | collective-permute-done | bytes 15392 | tf_op jit(solution)/shard_map/ppermute | solution.py:16
  190.0 17.7 %psum.15 = f32[8,320]{1,0:T(8,128)S(1)} all-reduce(f32[8,320]{1,0:T(8,128)S(1)} %fusion.144), channel_id=1, replica_groups=mesh['fine'=128,'tele'=4] {'tele'}, use_global_device_ids=true, to_apply=%region_10.14 | all-reduce | flops 2560 | bytes 20480 | tf_op jit(solution)/shard_map/psum | solution.py:152
  210.6 2.4 collective-permute-start.18
  213.1 6.0 %collective-permute-done.18 = bf16[8,6,80]{2,1,0:T(8,128)(2,1)S(1)} collective-permute-done((bf16[8,6,80]{2,1,0:T(8,128)(2,1)S(1)}, bf16[8,6,80]{2,1,0:T(8,128)(2,1)S(1)}, u32[]{:S(2)}, u32[]{:S(2)}) %collective-permute-start.18) | collective-permute-done | bytes 7712 | tf_op jit(solution)/shard_map/ppermute | solution.py:16
  223.7 2.4 collective-permute-start.20
  226.1 6.0 %collective-permute-done.20 = bf16[8,6,80]{2,1,0:T(8,128)(2,1)S(1)} collective-permute-done((bf16[8,6,80]{2,1,0:T(8,128)(2,1)S(1)}, bf16[8,6,80]{2,1,0:T(8,128)(2,1)S(1)}, u32[]{:S(2)}, u32[]{:S(2)}) %collective-permute-start.20) | collective-permute-done | bytes 7712 | tf_op jit(solution)/shard_map/ppermute | solution.py:16
  (179 shorter events, 52.6 us)
Async XLA Ops:
  6.5 31.5 %copy-start = (bf16[24,80,80]{2,1,0:T(8,128)(2,1)S(1)}, bf16[24,80,80]{2,1,0:T(8,128)(2,1)}, u32[]{:S(2)}) copy-start(bf16[24,80,80]{2,1,0:T(8,128)(2,1)} %param.33) | copy-start | bytes 921604
  6.5 29.8 %copy-start.5 = (s32[6]{0:T(128)S(1)}, s32[6]{0:T(128)}, u32[]{:S(2)}) copy-start(s32[6]{0:T(128)} %constant.277.clone) | copy-start | bytes 76
  6.5 32.1 %copy-start.2 = (f32[16,320]{1,0:T(8,128)S(1)}, f32[16,320]{1,0:T(8,128)}, u32[]{:S(2)}) copy-start(f32[16,320]{1,0:T(8,128)} %param.26) | copy-start | bytes 61444
  6.5 14.5 %copy-start.3 = (s32[16,6]{0,1:T(8,128)S(1)}, s32[16,6]{0,1:T(8,128)}, u32[]{:S(2)}) copy-start(s32[16,6]{0,1:T(8,128)} %param.28) | copy-start | bytes 1156
  6.5 14.5 %copy-start.6 = (s32[2,6]{1,0:T(2,128)S(1)}, s32[2,6]{1,0:T(2,128)}, u32[]{:S(2)}) copy-start(s32[2,6]{1,0:T(2,128)} %param.32) | copy-start | bytes 148
  6.5 14.5 %copy-start.7 = (s32[2,6]{1,0:T(2,128)S(1)}, s32[2,6]{1,0:T(2,128)}, u32[]{:S(2)}) copy-start(s32[2,6]{1,0:T(2,128)} %param.31) | copy-start | bytes 148
  6.6 30.1 %copy-start.8 = (s32[16]{0:T(128)S(1)}, s32[16]{0:T(128)}, u32[]{:S(2)}) copy-start(s32[16]{0:T(128)} %param.34) | copy-start | bytes 196
  6.6 30.3 %copy-start.4 = (s32[16,6]{0,1:T(8,128)S(1)}, s32[16,6]{0,1:T(8,128)}, u32[]{:S(2)}) copy-start(s32[16,6]{0,1:T(8,128)} %param.29) | copy-start | bytes 1156
  6.6 87.0 %all-gather.3.cloned.1.call-start = ((), (), s32[]{:S(2)}) async-start(), calls=%async_computation | async-start | bytes 2457600 | tf_op jit(solution)/shard_map/all_gather | solution.py:123
  11.3 26.0 %collective-permute-start.1 = (bf16[16,6,80]{2,1,0:T(8,128)(2,1)S(1)}, bf16[16,6,80]{2,1,0:T(8,128)(2,1)S(1)}, u32[]{:S(2)}, u32[]{:S(2)}) collective-permute-start(bf16[16,6,80]{2,1,0:T(8,128)(2,1)S(1)} %reshape.333), channel_id=1, source_target_pairs={{1,0},{2,1},{3,2},{4,3},{5,4},{6,5},{7,6},{8,7},{9,8},{10,9},{11,1... | collective-permute-start | bytes 46088 | tf_op jit(solution)/shard_map/ppermute | solution.py:16
  19.1 18.2 %collective-permute-start = (bf16[16,6,80]{2,1,0:T(8,128)(2,1)S(1)}, bf16[16,6,80]{2,1,0:T(8,128)(2,1)S(1)}, u32[]{:S(2)}, u32[]{:S(2)}) collective-permute-start(bf16[16,6,80]{2,1,0:T(8,128)(2,1)S(1)} %reshape.333), channel_id=1, source_target_pairs={{511,0},{0,1},{1,2},{2,3},{3,4},{4,5},{5,6},{6,7},{7,8},{8,9},{9,1... | collective-permute-start | bytes 46088 | tf_op jit(solution)/shard_map/ppermute | solution.py:16
  43.0 6.5 %collective-permute-start.3 = (bf16[16,6,80]{2,1,0:T(8,128)(2,1)S(1)}, bf16[16,6,80]{2,1,0:T(8,128)(2,1)S(1)}, u32[]{:S(2)}, u32[]{:S(2)}) collective-permute-start(bf16[16,6,80]{2,1,0:T(8,128)(2,1)S(1)} %reshape.337), channel_id=1, source_target_pairs={{1,0},{2,1},{3,2},{4,3},{5,4},{6,5},{7,6},{8,7},{9,8},{10,9},{11,1... | collective-permute-start | bytes 46088 | tf_op jit(solution)/shard_map/ppermute | solution.py:16
  45.5 8.8 %collective-permute-start.2 = (bf16[16,6,80]{2,1,0:T(8,128)(2,1)S(1)}, bf16[16,6,80]{2,1,0:T(8,128)(2,1)S(1)}, u32[]{:S(2)}, u32[]{:S(2)}) collective-permute-start(bf16[16,6,80]{2,1,0:T(8,128)(2,1)S(1)} %reshape.337), channel_id=1, source_target_pairs={{511,0},{0,1},{1,2},{2,3},{3,4},{4,5},{5,6},{6,7},{7,8},{8,9},{9,1... | collective-permute-start | bytes 46088 | tf_op jit(solution)/shard_map/ppermute | solution.py:16
  59.8 10.2 %collective-permute-start.5 = (bf16[16,6,80]{2,1,0:T(8,128)(2,1)S(1)}, bf16[16,6,80]{2,1,0:T(8,128)(2,1)S(1)}, u32[]{:S(2)}, u32[]{:S(2)}) collective-permute-start(bf16[16,6,80]{2,1,0:T(8,128)(2,1)S(1)} %reshape.341), channel_id=1, source_target_pairs={{1,0},{2,1},{3,2},{4,3},{5,4},{6,5},{7,6},{8,7},{9,8},{10,9},{11,1... | collective-permute-start | bytes 46088 | tf_op jit(solution)/shard_map/ppermute | solution.py:16
  68.0 5.8 %collective-permute-start.4 = (bf16[16,6,80]{2,1,0:T(8,128)(2,1)S(1)}, bf16[16,6,80]{2,1,0:T(8,128)(2,1)S(1)}, u32[]{:S(2)}, u32[]{:S(2)}) collective-permute-start(bf16[16,6,80]{2,1,0:T(8,128)(2,1)S(1)} %reshape.341), channel_id=1, source_target_pairs={{511,0},{0,1},{1,2},{2,3},{3,4},{4,5},{5,6},{6,7},{7,8},{8,9},{9,1... | collective-permute-start | bytes 46088 | tf_op jit(solution)/shard_map/ppermute | solution.py:16
  93.6 29.3 %copy-start.1 = (bf16[8,320,320]{2,1,0:T(8,128)(2,1)S(1)}, bf16[8,320,320]{2,1,0:T(8,128)(2,1)}, u32[]{:S(2)}) copy-start(bf16[8,320,320]{2,1,0:T(8,128)(2,1)} %all-gather.3.cloned.1.call-done) | copy-start | bytes 4915204
  96.3 4.4 %collective-permute-start.7 = (bf16[8,6,80]{2,1,0:T(8,128)(2,1)S(1)}, bf16[8,6,80]{2,1,0:T(8,128)(2,1)S(1)}, u32[]{:S(2)}, u32[]{:S(2)}) collective-permute-start(bf16[8,6,80]{2,1,0:T(8,128)(2,1)S(1)} %reshape.345), channel_id=1, source_target_pairs={{4,0},{8,4},{12,8},{16,12},{20,16},{24,20},{28,24},{32,28},{36,32}... | collective-permute-start | bytes 23048 | tf_op jit(solution)/shard_map/ppermute | solution.py:16
  98.2 8.4 %collective-permute-start.6 = (bf16[8,6,80]{2,1,0:T(8,128)(2,1)S(1)}, bf16[8,6,80]{2,1,0:T(8,128)(2,1)S(1)}, u32[]{:S(2)}, u32[]{:S(2)}) collective-permute-start(bf16[8,6,80]{2,1,0:T(8,128)(2,1)S(1)} %reshape.345), channel_id=1, source_target_pairs={{508,0},{0,4},{4,8},{8,12},{12,16},{16,20},{20,24},{24,28},{28,32}... | collective-permute-start | bytes 23048 | tf_op jit(solution)/shard_map/ppermute | solution.py:16
  110.9 4.4 %collective-permute-start.9 = (bf16[8,6,80]{2,1,0:T(8,128)(2,1)S(1)}, bf16[8,6,80]{2,1,0:T(8,128)(2,1)S(1)}, u32[]{:S(2)}, u32[]{:S(2)}) collective-permute-start(bf16[8,6,80]{2,1,0:T(8,128)(2,1)S(1)} %reshape.349), channel_id=1, source_target_pairs={{4,0},{8,4},{12,8},{16,12},{20,16},{24,20},{28,24},{32,28},{36,32}... | collective-permute-start | bytes 23048 | tf_op jit(solution)/shard_map/ppermute | solution.py:16
  112.8 8.4 %collective-permute-start.8 = (bf16[8,6,80]{2,1,0:T(8,128)(2,1)S(1)}, bf16[8,6,80]{2,1,0:T(8,128)(2,1)S(1)}, u32[]{:S(2)}, u32[]{:S(2)}) collective-permute-start(bf16[8,6,80]{2,1,0:T(8,128)(2,1)S(1)} %reshape.349), channel_id=1, source_target_pairs={{508,0},{0,4},{4,8},{8,12},{12,16},{16,20},{20,24},{24,28},{28,32}... | collective-permute-start | bytes 23048 | tf_op jit(solution)/shard_map/ppermute | solution.py:16
  124.5 5.9 %collective-permute-start.11 = (bf16[16,6,80]{2,1,0:T(8,128)(2,1)S(1)}, bf16[16,6,80]{2,1,0:T(8,128)(2,1)S(1)}, u32[]{:S(2)}, u32[]{:S(2)}) collective-permute-start(bf16[16,6,80]{2,1,0:T(8,128)(2,1)S(1)} %reshape.353), channel_id=1, source_target_pairs={{1,0},{2,1},{3,2},{4,3},{5,4},{6,5},{7,6},{8,7},{9,8},{10,9},{11,1... | collective-permute-start | bytes 46088 | tf_op jit(solution)/shard_map/ppermute | solution.py:16
  127.9 5.8 %collective-permute-start.10 = (bf16[16,6,80]{2,1,0:T(8,128)(2,1)S(1)}, bf16[16,6,80]{2,1,0:T(8,128)(2,1)S(1)}, u32[]{:S(2)}, u32[]{:S(2)}) collective-permute-start(bf16[16,6,80]{2,1,0:T(8,128)(2,1)S(1)} %reshape.353), channel_id=1, source_target_pairs={{511,0},{0,1},{1,2},{2,3},{3,4},{4,5},{5,6},{6,7},{7,8},{8,9},{9,1... | collective-permute-start | bytes 46088 | tf_op jit(solution)/shard_map/ppermute | solution.py:16
  139.1 9.0 %collective-permute-start.13 = (bf16[16,6,80]{2,1,0:T(8,128)(2,1)S(1)}, bf16[16,6,80]{2,1,0:T(8,128)(2,1)S(1)}, u32[]{:S(2)}, u32[]{:S(2)}) collective-permute-start(bf16[16,6,80]{2,1,0:T(8,128)(2,1)S(1)} %reshape.357), channel_id=1, source_target_pairs={{1,0},{2,1},{3,2},{4,3},{5,4},{6,5},{7,6},{8,7},{9,8},{10,9},{11,1... | collective-permute-start | bytes 46088 | tf_op jit(solution)/shard_map/ppermute | solution.py:16
  146.0 5.8 %collective-permute-start.12 = (bf16[16,6,80]{2,1,0:T(8,128)(2,1)S(1)}, bf16[16,6,80]{2,1,0:T(8,128)(2,1)S(1)}, u32[]{:S(2)}, u32[]{:S(2)}) collective-permute-start(bf16[16,6,80]{2,1,0:T(8,128)(2,1)S(1)} %reshape.357), channel_id=1, source_target_pairs={{511,0},{0,1},{1,2},{2,3},{3,4},{4,5},{5,6},{6,7},{7,8},{8,9},{9,1... | collective-permute-start | bytes 46088 | tf_op jit(solution)/shard_map/ppermute | solution.py:16
  157.3 8.7 %collective-permute-start.15 = (bf16[16,6,80]{2,1,0:T(8,128)(2,1)S(1)}, bf16[16,6,80]{2,1,0:T(8,128)(2,1)S(1)}, u32[]{:S(2)}, u32[]{:S(2)}) collective-permute-start(bf16[16,6,80]{2,1,0:T(8,128)(2,1)S(1)} %reshape.361), channel_id=1, source_target_pairs={{1,0},{2,1},{3,2},{4,3},{5,4},{6,5},{7,6},{8,7},{9,8},{10,9},{11,1... | collective-permute-start | bytes 46088 | tf_op jit(solution)/shard_map/ppermute | solution.py:16
  164.1 5.8 %collective-permute-start.14 = (bf16[16,6,80]{2,1,0:T(8,128)(2,1)S(1)}, bf16[16,6,80]{2,1,0:T(8,128)(2,1)S(1)}, u32[]{:S(2)}, u32[]{:S(2)}) collective-permute-start(bf16[16,6,80]{2,1,0:T(8,128)(2,1)S(1)} %reshape.361), channel_id=1, source_target_pairs={{511,0},{0,1},{1,2},{2,3},{3,4},{4,5},{5,6},{6,7},{7,8},{8,9},{9,1... | collective-permute-start | bytes 46088 | tf_op jit(solution)/shard_map/ppermute | solution.py:16
  175.3 8.7 %collective-permute-start.17 = (bf16[16,6,80]{2,1,0:T(8,128)(2,1)S(1)}, bf16[16,6,80]{2,1,0:T(8,128)(2,1)S(1)}, u32[]{:S(2)}, u32[]{:S(2)}) collective-permute-start(bf16[16,6,80]{2,1,0:T(8,128)(2,1)S(1)} %reshape.365), channel_id=1, source_target_pairs={{1,0},{2,1},{3,2},{4,3},{5,4},{6,5},{7,6},{8,7},{9,8},{10,9},{11,1... | collective-permute-start | bytes 46088 | tf_op jit(solution)/shard_map/ppermute | solution.py:16
  182.1 5.9 %collective-permute-start.16 = (bf16[16,6,80]{2,1,0:T(8,128)(2,1)S(1)}, bf16[16,6,80]{2,1,0:T(8,128)(2,1)S(1)}, u32[]{:S(2)}, u32[]{:S(2)}) collective-permute-start(bf16[16,6,80]{2,1,0:T(8,128)(2,1)S(1)} %reshape.365), channel_id=1, source_target_pairs={{511,0},{0,1},{1,2},{2,3},{3,4},{4,5},{5,6},{6,7},{7,8},{8,9},{9,1... | collective-permute-start | bytes 46088 | tf_op jit(solution)/shard_map/ppermute | solution.py:16
  208.7 4.3 %collective-permute-start.19 = (bf16[8,6,80]{2,1,0:T(8,128)(2,1)S(1)}, bf16[8,6,80]{2,1,0:T(8,128)(2,1)S(1)}, u32[]{:S(2)}, u32[]{:S(2)}) collective-permute-start(bf16[8,6,80]{2,1,0:T(8,128)(2,1)S(1)} %reshape.369), channel_id=1, source_target_pairs={{4,0},{8,4},{12,8},{16,12},{20,16},{24,20},{28,24},{32,28},{36,32}... | collective-permute-start | bytes 23048 | tf_op jit(solution)/shard_map/ppermute | solution.py:16
  210.6 8.4 %collective-permute-start.18 = (bf16[8,6,80]{2,1,0:T(8,128)(2,1)S(1)}, bf16[8,6,80]{2,1,0:T(8,128)(2,1)S(1)}, u32[]{:S(2)}, u32[]{:S(2)}) collective-permute-start(bf16[8,6,80]{2,1,0:T(8,128)(2,1)S(1)} %reshape.369), channel_id=1, source_target_pairs={{508,0},{0,4},{4,8},{8,12},{12,16},{16,20},{20,24},{24,28},{28,32}... | collective-permute-start | bytes 23048 | tf_op jit(solution)/shard_map/ppermute | solution.py:16
  221.8 4.3 %collective-permute-start.21 = (bf16[8,6,80]{2,1,0:T(8,128)(2,1)S(1)}, bf16[8,6,80]{2,1,0:T(8,128)(2,1)S(1)}, u32[]{:S(2)}, u32[]{:S(2)}) collective-permute-start(bf16[8,6,80]{2,1,0:T(8,128)(2,1)S(1)} %reshape.373), channel_id=1, source_target_pairs={{4,0},{8,4},{12,8},{16,12},{20,16},{24,20},{28,24},{32,28},{36,32}... | collective-permute-start | bytes 23048 | tf_op jit(solution)/shard_map/ppermute | solution.py:16
  223.7 8.4 %collective-permute-start.20 = (bf16[8,6,80]{2,1,0:T(8,128)(2,1)S(1)}, bf16[8,6,80]{2,1,0:T(8,128)(2,1)S(1)}, u32[]{:S(2)}, u32[]{:S(2)}) collective-permute-start(bf16[8,6,80]{2,1,0:T(8,128)(2,1)S(1)} %reshape.373), channel_id=1, source_target_pairs={{508,0},{0,4},{4,8},{8,12},{12,16},{16,20},{20,24},{24,28},{28,32}... | collective-permute-start | bytes 23048 | tf_op jit(solution)/shard_map/ppermute | solution.py:16
Sparse Core Ops, SparseCore 0:
  21.2 38.3 all-gather.2
where the time goes:
time: 244 us; the launch traced here: 243 us
  starting transfers between devices  75.3 us (31%)
  blocking collectives  50.6 us (21%)
  waiting for transfers between devices  47.8 us (20%)
  matrix products  40.2 us (16%)
  between operations  14.2 us (6%)
  local copies, waits for them, and re-layouts  12.1 us (5%)
    ppermute x22, starting transfers between devices, passed_along(): return lax.ppermute(block, axis, route)  75.3 us
    ppermute x22, waiting for transfers between devices, passed_along(): return lax.ppermute(block, axis, route)  47.8 us
    psum x2, blocking collectives, shards(): restricted = lax.psum(partial_sum, 'tele')  35.5 us
    dot_general x12, matrix products, apply_inverse(): jnp.einsum('nij,nj->ni', inverse, lowered, preferred_element_type=jnp.flo...  27.4 us
    all_gather x1, blocking collectives, shards(): lax.all_gather(jnp.concatenate([coarse_links, coarse_faces], axis=1), 'te...  15.2 us
    gather x11, local copies, waits for them, and re-layouts, neighbour_rows(): jnp.take(trace_pool, row_index.reshape(-1), axis=0)  7.19 us
  transfers between devices with their start and end apart: 23, of which 11 were waited for; matrix products, arithmetic and copies ran while one was open for 6% of the time, Pallas kernels for 0%

commit v1 on v0

--- a/solution.py
+++ b/solution.py
@@ -8,6 +8,15 @@
 SWEEPS = 3
 CYCLES = 2
 OPPOSITE = (1, 0, 3, 2, 5, 4)
+
+
+def added_up(value, mesh_axis):
+    size = lax.axis_size(mesh_axis)
+    summed, far = (value, 1)
+    while far < size:
+        summed = summed + lax.ppermute(summed, mesh_axis, [(i, i ^ far) for i in range(size)])
+        far = 2 * far
+    return summed
 
 
 def passed_along(block, axis, distance):
@@ -149,7 +158,7 @@
         partial_sum = jnp.dot(
             member.T, residual, precision=lax.Precision.HIGHEST, preferred_element_type=jnp.float32
         )
-        restricted = lax.psum(partial_sum, "tele")
+        restricted = added_up(partial_sum, "tele")
         coarse_state = apply_inverse(block_inverse, restricted.astype(jnp.bfloat16))
         for sweep_index in range(SWEEPS - 1):
             coupled_coarse = coarse_coupling(

time: 244 us -> 239 us (0.980)
  blocking collectives: 50.6 us -> 15.2 us
  starting transfers between devices: 75.3 us -> 92.5 us
  waiting for transfers between devices: 47.8 us -> 61.9 us
    psum x2 -> x0, blocking collectives: 35.5 us -> none  [shards(): restricted = lax.psum(partial_sum, 'tele')]
    ppermute x0 -> x4, starting transfers between devices: none -> 17.4 us  [added_up(): lax.ppermute(summed, mesh_axis, [(i, i ^ far) for i in range(size)])]
    ppermute x0 -> x4, waiting for transfers between devices: none -> 13.6 us  [added_up(): lax.ppermute(summed, mesh_axis, [(i, i ^ far) for i in range(size)])]
  transfers between devices with their start and end apart: 23 -> 27, of which waited for: 11 -> 15; matrix products, arithmetic and copies ran while one was open for 6% -> 6% of each run, Pallas kernels for 0% -> 0%
where the time goes in v1:
time: 239 us; the launch traced here: 238 us
  starting transfers between devices  92.5 us (39%)
  waiting for transfers between devices  61.9 us (26%)
  matrix products  40.3 us (17%)
  blocking collectives  15.2 us (6%)
  between operations  14.2 us (6%)
  local copies, waits for them, and re-layouts  12.1 us (5%)
    ppermute x22, starting transfers between devices, passed_along(): return lax.ppermute(block, axis, route)  75.1 us
    ppermute x22, waiting for transfers between devices, passed_along(): return lax.ppermute(block, axis, route)  48.3 us
    dot_general x12, matrix products, apply_inverse(): jnp.einsum('nij,nj->ni', inverse, lowered, preferred_element_type=jnp.flo...  27.4 us
    ppermute x4, starting transfers between devices, added_up(): lax.ppermute(summed, mesh_axis, [(i, i ^ far) for i in range(size)])  17.4 us
    all_gather x1, blocking collectives, shards(): lax.all_gather(jnp.concatenate([coarse_links, coarse_faces], axis=1), 'te...  15.2 us
    ppermute x4, waiting for transfers between devices, added_up(): lax.ppermute(summed, mesh_axis, [(i, i ^ far) for i in range(size)])  13.6 us
    gather x11, local copies, waits for them, and re-layouts, neighbour_rows(): jnp.take(trace_pool, row_index.reshape(-1), axis=0)  7.19 us
  transfers between devices with their start and end apart: 27, of which 15 were waited for; matrix products, arithmetic and copies ran while one was open for 6% of the time, Pallas kernels for 0%

profile of v1, /device:TPU:2, one launch (start us, length us, event | category | flops | bytes accessed | tf_op | source)
XLA Modules:
  0.0 238.4 jit_solution(3548786121792401293)
XLA Ops:
  7.5 3.3 %fusion.76 = f32[16,1,320]{2,1,0:T(1,128)S(1)} fusion(bf16[16,320,320]{2,1,0:T(8,128)(2,1)} %param.27, bf16[16,320,1]{1,0,2:T(8,128)(2,1)S(1)} %convert_bitcast_fusion), kind=kOutput, calls=%fused_computation.136 | convolution fusion | flops 3276800 | bytes 3307520 | tf_op jit(solution)/shard_map/nij,nj->ni/dot_general | solution.py:107
  11.2 7.8 %collective-permute-start.1 = (bf16[16,6,80]{2,1,0:T(8,128)(2,1)S(1)}, bf16[16,6,80]{2,1,0:T(8,128)(2,1)S(1)}, u32[]{:S(2)}, u32[]{:S(2)}) collective-permute-start(bf16[16,6,80]{2,1,0:T(8,128)(2,1)S(1)} %reshape.333), channel_id=1, source_target_pairs={{1,0},{2,1},{3,2},{4,3},{5,4},{6,5},{7,6},{8,7},{9,8},{10,9},{11,1... | collective-permute-start | bytes 46088 | tf_op jit(solution)/shard_map/ppermute | solution.py:25
  21.1 15.2 %all-gather = s32[4,2,12]{2,1,0:T(2,128)S(1)} all-gather(s32[1,2,12]{2,1,0:T(2,128)S(1)} %add_bitcast_fusion), channel_id=1, replica_groups=mesh['fine'=128,'tele'=4] {'tele'}, dimensions={0}, use_global_device_ids=true | all-gather | bytes 480 | tf_op jit(solution)/shard_map/all_gather | solution.py:133
  38.9 3.5 %fusion.73 = f32[16,1,320]{2,1,0:T(1,128)S(1)} fusion(bf16[16,320,320]{2,1,0:T(8,128)(2,1)} %param.27, bf16[16,320,1]{1,0,2:T(8,128)(2,1)S(1)} %fusion.18), kind=kOutput, calls=%fused_computation.133 | convolution fusion | flops 3276800 | bytes 3307520 | tf_op jit(solution)/shard_map/nij,nj->ni/dot_general | solution.py:107
  42.9 2.7 %collective-permute-start.3 = (bf16[16,6,80]{2,1,0:T(8,128)(2,1)S(1)}, bf16[16,6,80]{2,1,0:T(8,128)(2,1)S(1)}, u32[]{:S(2)}, u32[]{:S(2)}) collective-permute-start(bf16[16,6,80]{2,1,0:T(8,128)(2,1)S(1)} %reshape.337), channel_id=1, source_target_pairs={{1,0},{2,1},{3,2},{4,3},{5,4},{6,5},{7,6},{8,7},{9,8},{10,9},{11,1... | collective-permute-start | bytes 46088 | tf_op jit(solution)/shard_map/ppermute | solution.py:25
  45.5 3.2 %collective-permute-start.2 = (bf16[16,6,80]{2,1,0:T(8,128)(2,1)S(1)}, bf16[16,6,80]{2,1,0:T(8,128)(2,1)S(1)}, u32[]{:S(2)}, u32[]{:S(2)}) collective-permute-start(bf16[16,6,80]{2,1,0:T(8,128)(2,1)S(1)} %reshape.337), channel_id=1, source_target_pairs={{511,0},{0,1},{1,2},{2,3},{3,4},{4,5},{5,6},{6,7},{7,8},{8,9},{9,1... | collective-permute-start | bytes 46088 | tf_op jit(solution)/shard_map/ppermute | solution.py:25
  49.3 4.9 %collective-permute-done.2 = bf16[16,6,80]{2,1,0:T(8,128)(2,1)S(1)} collective-permute-done((bf16[16,6,80]{2,1,0:T(8,128)(2,1)S(1)}, bf16[16,6,80]{2,1,0:T(8,128)(2,1)S(1)}, u32[]{:S(2)}, u32[]{:S(2)}) %collective-permute-start.2) | collective-permute-done | bytes 15392 | tf_op jit(solution)/shard_map/ppermute | solution.py:25
  55.9 3.3 %fusion.70 = f32[16,1,320]{2,1,0:T(1,128)S(1)} fusion(bf16[16,320,320]{2,1,0:T(8,128)(2,1)} %param.27, bf16[16,320,1]{1,0,2:T(8,128)(2,1)S(1)} %bitcast.137), kind=kOutput, calls=%fused_computation.130 | convolution fusion | flops 3276800 | bytes 3307520 | tf_op jit(solution)/shard_map/nij,nj->ni/dot_general | solution.py:107
  59.7 8.2 %collective-permute-start.5 = (bf16[16,6,80]{2,1,0:T(8,128)(2,1)S(1)}, bf16[16,6,80]{2,1,0:T(8,128)(2,1)S(1)}, u32[]{:S(2)}, u32[]{:S(2)}) collective-permute-start(bf16[16,6,80]{2,1,0:T(8,128)(2,1)S(1)} %reshape.341), channel_id=1, source_target_pairs={{1,0},{2,1},{3,2},{4,3},{5,4},{6,5},{7,6},{8,7},{9,8},{10,9},{11,1... | collective-permute-start | bytes 46088 | tf_op jit(solution)/shard_map/ppermute | solution.py:25
  69.9 3.8 %collective-permute-done.4 = bf16[16,6,80]{2,1,0:T(8,128)(2,1)S(1)} collective-permute-done((bf16[16,6,80]{2,1,0:T(8,128)(2,1)S(1)}, bf16[16,6,80]{2,1,0:T(8,128)(2,1)S(1)}, u32[]{:S(2)}, u32[]{:S(2)}) %collective-permute-start.4) | collective-permute-done | bytes 15392 | tf_op jit(solution)/shard_map/ppermute | solution.py:25
  75.7 6.8 %collective-permute-start.6 = (f32[8,320]{1,0:T(8,128)S(1)}, f32[8,320]{1,0:T(8,128)S(1)}, u32[]{:S(2)}, u32[]{:S(2)}) collective-permute-start(f32[8,320]{1,0:T(8,128)S(1)} %fusion.145), channel_id=1, source_target_pairs={{0,1},{1,0},{2,3},{3,2},{4,5},{5,4},{6,7},{7,6},{8,9},{9,8},{10,11... | collective-permute-start | bytes 30728 | tf_op jit(solution)/shard_map/ppermute | solution.py:17
  86.0 5.2 %collective-permute-done.7 = f32[8,320]{1,0:T(8,128)S(1)} collective-permute-done((f32[8,320]{1,0:T(8,128)S(1)}, f32[8,320]{1,0:T(8,128)S(1)}, u32[]{:S(2)}, u32[]{:S(2)}) %collective-permute-start.7) | collective-permute-done | bytes 10272 | tf_op jit(solution)/shard_map/ppermute | solution.py:17
  95.9 2.4 %collective-permute-start.8 = (bf16[8,6,80]{2,1,0:T(8,128)(2,1)S(1)}, bf16[8,6,80]{2,1,0:T(8,128)(2,1)S(1)}, u32[]{:S(2)}, u32[]{:S(2)}) collective-permute-start(bf16[8,6,80]{2,1,0:T(8,128)(2,1)S(1)} %reshape.345), channel_id=1, source_target_pairs={{508,0},{0,4},{4,8},{8,12},{12,16},{16,20},{20,24},{24,28},{28,32}... | collective-permute-start | bytes 23048 | tf_op jit(solution)/shard_map/ppermute | solution.py:25
  98.4 5.9 %collective-permute-done.8 = bf16[8,6,80]{2,1,0:T(8,128)(2,1)S(1)} collective-permute-done((bf16[8,6,80]{2,1,0:T(8,128)(2,1)S(1)}, bf16[8,6,80]{2,1,0:T(8,128)(2,1)S(1)}, u32[]{:S(2)}, u32[]{:S(2)}) %collective-permute-start.8) | collective-permute-done | bytes 7712 | tf_op jit(solution)/shard_map/ppermute | solution.py:25
  112.9 5.9 %collective-permute-done.10 = bf16[8,6,80]{2,1,0:T(8,128)(2,1)S(1)} collective-permute-done((bf16[8,6,80]{2,1,0:T(8,128)(2,1)S(1)}, bf16[8,6,80]{2,1,0:T(8,128)(2,1)S(1)}, u32[]{:S(2)}, u32[]{:S(2)}) %collective-permute-start.10) | collective-permute-done | bytes 7712 | tf_op jit(solution)/shard_map/ppermute | solution.py:25
  122.2 3.9 %collective-permute-start.13 = (bf16[16,6,80]{2,1,0:T(8,128)(2,1)S(1)}, bf16[16,6,80]{2,1,0:T(8,128)(2,1)S(1)}, u32[]{:S(2)}, u32[]{:S(2)}) collective-permute-start(bf16[16,6,80]{2,1,0:T(8,128)(2,1)S(1)} %reshape.353), channel_id=1, source_target_pairs={{1,0},{2,1},{3,2},{4,3},{5,4},{6,5},{7,6},{8,7},{9,8},{10,9},{11,1... | collective-permute-start | bytes 46088 | tf_op jit(solution)/shard_map/ppermute | solution.py:25
  128.0 3.9 %collective-permute-done.12 = bf16[16,6,80]{2,1,0:T(8,128)(2,1)S(1)} collective-permute-done((bf16[16,6,80]{2,1,0:T(8,128)(2,1)S(1)}, bf16[16,6,80]{2,1,0:T(8,128)(2,1)S(1)}, u32[]{:S(2)}, u32[]{:S(2)}) %collective-permute-start.12) | collective-permute-done | bytes 15392 | tf_op jit(solution)/shard_map/ppermute | solution.py:25
  133.6 3.3 %fusion.68 = f32[16,1,320]{2,1,0:T(1,128)S(1)} fusion(bf16[16,320,320]{2,1,0:T(8,128)(2,1)} %param.27, bf16[16,320,1]{1,0,2:T(8,128)(2,1)S(1)} %fusion.17), kind=kOutput, calls=%fused_computation.128 | convolution fusion | flops 3276800 | bytes 3307520 | tf_op jit(solution)/shard_map/nij,nj->ni/dot_general | solution.py:107
  137.3 6.8 %collective-permute-start.15 = (bf16[16,6,80]{2,1,0:T(8,128)(2,1)S(1)}, bf16[16,6,80]{2,1,0:T(8,128)(2,1)S(1)}, u32[]{:S(2)}, u32[]{:S(2)}) collective-permute-start(bf16[16,6,80]{2,1,0:T(8,128)(2,1)S(1)} %reshape.357), channel_id=1, source_target_pairs={{1,0},{2,1},{3,2},{4,3},{5,4},{6,5},{7,6},{8,7},{9,8},{10,9},{11,1... | collective-permute-start | bytes 46088 | tf_op jit(solution)/shard_map/ppermute | solution.py:25
  146.1 3.9 %collective-permute-done.14 = bf16[16,6,80]{2,1,0:T(8,128)(2,1)S(1)} collective-permute-done((bf16[16,6,80]{2,1,0:T(8,128)(2,1)S(1)}, bf16[16,6,80]{2,1,0:T(8,128)(2,1)S(1)}, u32[]{:S(2)}, u32[]{:S(2)}) %collective-permute-start.14) | collective-permute-done | bytes 15392 | tf_op jit(solution)/shard_map/ppermute | solution.py:25
  151.6 3.3 %fusion.65 = f32[16,1,320]{2,1,0:T(1,128)S(1)} fusion(bf16[16,320,320]{2,1,0:T(8,128)(2,1)} %param.27, bf16[16,320,1]{1,0,2:T(8,128)(2,1)S(1)} %fusion.16), kind=kOutput, calls=%fused_computation.125 | convolution fusion | flops 3276800 | bytes 3307520 | tf_op jit(solution)/shard_map/nij,nj->ni/dot_general | solution.py:107
  155.4 6.8 %collective-permute-start.17 = (bf16[16,6,80]{2,1,0:T(8,128)(2,1)S(1)}, bf16[16,6,80]{2,1,0:T(8,128)(2,1)S(1)}, u32[]{:S(2)}, u32[]{:S(2)}) collective-permute-start(bf16[16,6,80]{2,1,0:T(8,128)(2,1)S(1)} %reshape.361), channel_id=1, source_target_pairs={{1,0},{2,1},{3,2},{4,3},{5,4},{6,5},{7,6},{8,7},{9,8},{10,9},{11,1... | collective-permute-start | bytes 46088 | tf_op jit(solution)/shard_map/ppermute | solution.py:25
  164.3 3.7 %collective-permute-done.16 = bf16[16,6,80]{2,1,0:T(8,128)(2,1)S(1)} collective-permute-done((bf16[16,6,80]{2,1,0:T(8,128)(2,1)S(1)}, bf16[16,6,80]{2,1,0:T(8,128)(2,1)S(1)}, u32[]{:S(2)}, u32[]{:S(2)}) %collective-permute-start.16) | collective-permute-done | bytes 15392 | tf_op jit(solution)/shard_map/ppermute | solution.py:25
  169.7 3.3 %fusion.62 = f32[16,1,320]{2,1,0:T(1,128)S(1)} fusion(bf16[16,320,320]{2,1,0:T(8,128)(2,1)} %param.27, bf16[16,320,1]{1,0,2:T(8,128)(2,1)S(1)} %bitcast.138), kind=kOutput, calls=%fused_computation.122 | convolution fusion | flops 3276800 | bytes 3307520 | tf_op jit(solution)/shard_map/nij,nj->ni/dot_general | solution.py:107
  173.4 6.8 %collective-permute-start.19 = (bf16[16,6,80]{2,1,0:T(8,128)(2,1)S(1)}, bf16[16,6,80]{2,1,0:T(8,128)(2,1)S(1)}, u32[]{:S(2)}, u32[]{:S(2)}) collective-permute-start(bf16[16,6,80]{2,1,0:T(8,128)(2,1)S(1)} %reshape.365), channel_id=1, source_target_pairs={{1,0},{2,1},{3,2},{4,3},{5,4},{6,5},{7,6},{8,7},{9,8},{10,9},{11,1... | collective-permute-start | bytes 46088 | tf_op jit(solution)/shard_map/ppermute | solution.py:25
  182.2 3.9 %collective-permute-done.18 = bf16[16,6,80]{2,1,0:T(8,128)(2,1)S(1)} collective-permute-done((bf16[16,6,80]{2,1,0:T(8,128)(2,1)S(1)}, bf16[16,6,80]{2,1,0:T(8,128)(2,1)S(1)}, u32[]{:S(2)}, u32[]{:S(2)}) %collective-permute-start.18) | collective-permute-done | bytes 15392 | tf_op jit(solution)/shard_map/ppermute | solution.py:25
  188.0 6.8 %collective-permute-start.20 = (f32[8,320]{1,0:T(8,128)S(1)}, f32[8,320]{1,0:T(8,128)S(1)}, u32[]{:S(2)}, u32[]{:S(2)}) collective-permute-start(f32[8,320]{1,0:T(8,128)S(1)} %fusion.144), channel_id=1, source_target_pairs={{0,1},{1,0},{2,3},{3,2},{4,5},{5,4},{6,7},{7,6},{8,9},{9,8},{10,11... | collective-permute-start | bytes 30728 | tf_op jit(solution)/shard_map/ppermute | solution.py:17
  198.4 5.2 %collective-permute-done.21 = f32[8,320]{1,0:T(8,128)S(1)} collective-permute-done((f32[8,320]{1,0:T(8,128)S(1)}, f32[8,320]{1,0:T(8,128)S(1)}, u32[]{:S(2)}, u32[]{:S(2)}) %collective-permute-start.21) | collective-permute-done | bytes 10272 | tf_op jit(solution)/shard_map/ppermute | solution.py:17
  206.5 2.4 %collective-permute-start.22 = (bf16[8,6,80]{2,1,0:T(8,128)(2,1)S(1)}, bf16[8,6,80]{2,1,0:T(8,128)(2,1)S(1)}, u32[]{:S(2)}, u32[]{:S(2)}) collective-permute-start(bf16[8,6,80]{2,1,0:T(8,128)(2,1)S(1)} %reshape.369), channel_id=1, source_target_pairs={{508,0},{0,4},{4,8},{8,12},{12,16},{16,20},{20,24},{24,28},{28,32}... | collective-permute-start | bytes 23048 | tf_op jit(solution)/shard_map/ppermute | solution.py:25
  208.9 6.0 %collective-permute-done.22 = bf16[8,6,80]{2,1,0:T(8,128)(2,1)S(1)} collective-permute-done((bf16[8,6,80]{2,1,0:T(8,128)(2,1)S(1)}, bf16[8,6,80]{2,1,0:T(8,128)(2,1)S(1)}, u32[]{:S(2)}, u32[]{:S(2)}) %collective-permute-start.22) | collective-permute-done | bytes 7712 | tf_op jit(solution)/shard_map/ppermute | solution.py:25
  219.6 2.4 %collective-permute-start.24 = (bf16[8,6,80]{2,1,0:T(8,128)(2,1)S(1)}, bf16[8,6,80]{2,1,0:T(8,128)(2,1)S(1)}, u32[]{:S(2)}, u32[]{:S(2)}) collective-permute-start(bf16[8,6,80]{2,1,0:T(8,128)(2,1)S(1)} %reshape.373), channel_id=1, source_target_pairs={{508,0},{0,4},{4,8},{8,12},{12,16},{16,20},{20,24},{24,28},{28,32}... | collective-permute-start | bytes 23048 | tf_op jit(solution)/shard_map/ppermute | solution.py:25
  222.0 6.0 %collective-permute-done.24 = bf16[8,6,80]{2,1,0:T(8,128)(2,1)S(1)} collective-permute-done((bf16[8,6,80]{2,1,0:T(8,128)(2,1)S(1)}, bf16[8,6,80]{2,1,0:T(8,128)(2,1)S(1)}, u32[]{:S(2)}, u32[]{:S(2)}) %collective-permute-start.24) | collective-permute-done | bytes 7712 | tf_op jit(solution)/shard_map/ppermute | solution.py:25
  (187 shorter events, 64.0 us)
Async XLA Ops:
  6.5 31.4 %copy-start = (bf16[24,80,80]{2,1,0:T(8,128)(2,1)S(1)}, bf16[24,80,80]{2,1,0:T(8,128)(2,1)}, u32[]{:S(2)}) copy-start(bf16[24,80,80]{2,1,0:T(8,128)(2,1)} %param.33) | copy-start | bytes 921604
  6.5 29.8 %copy-start.5 = (s32[6]{0:T(128)S(1)}, s32[6]{0:T(128)}, u32[]{:S(2)}) copy-start(s32[6]{0:T(128)} %constant.277.clone) | copy-start | bytes 76
  6.5 32.0 %copy-start.2 = (f32[16,320]{1,0:T(8,128)S(1)}, f32[16,320]{1,0:T(8,128)}, u32[]{:S(2)}) copy-start(f32[16,320]{1,0:T(8,128)} %param.26) | copy-start | bytes 61444
  6.6 30.2 %copy-start.4 = (s32[16,6]{0,1:T(8,128)S(1)}, s32[16,6]{0,1:T(8,128)}, u32[]{:S(2)}) copy-start(s32[16,6]{0,1:T(8,128)} %param.29) | copy-start | bytes 1156
  6.6 84.6 %all-gather.3.cloned.1.call-start = ((), (), s32[]{:S(2)}) async-start(), calls=%async_computation | async-start | bytes 2457600 | tf_op jit(solution)/shard_map/all_gather | solution.py:132
  10.8 37.9 %copy-start.8 = (s32[16]{0:T(128)S(1)}, s32[16]{0:T(128)}, u32[]{:S(2)}) copy-start(s32[16]{0:T(128)} %param.34) | copy-start | bytes 196
  11.2 25.9 %collective-permute-start.1 = (bf16[16,6,80]{2,1,0:T(8,128)(2,1)S(1)}, bf16[16,6,80]{2,1,0:T(8,128)(2,1)S(1)}, u32[]{:S(2)}, u32[]{:S(2)}) collective-permute-start(bf16[16,6,80]{2,1,0:T(8,128)(2,1)S(1)} %reshape.333), channel_id=1, source_target_pairs={{1,0},{2,1},{3,2},{4,3},{5,4},{6,5},{7,6},{8,7},{9,8},{10,9},{11,1... | collective-permute-start | bytes 46088 | tf_op jit(solution)/shard_map/ppermute | solution.py:25
  19.1 18.1 %collective-permute-start = (bf16[16,6,80]{2,1,0:T(8,128)(2,1)S(1)}, bf16[16,6,80]{2,1,0:T(8,128)(2,1)S(1)}, u32[]{:S(2)}, u32[]{:S(2)}) collective-permute-start(bf16[16,6,80]{2,1,0:T(8,128)(2,1)S(1)} %reshape.333), channel_id=1, source_target_pairs={{511,0},{0,1},{1,2},{2,3},{3,4},{4,5},{5,6},{6,7},{7,8},{8,9},{9,1... | collective-permute-start | bytes 46088 | tf_op jit(solution)/shard_map/ppermute | solution.py:25
  42.9 6.5 %collective-permute-start.3 = (bf16[16,6,80]{2,1,0:T(8,128)(2,1)S(1)}, bf16[16,6,80]{2,1,0:T(8,128)(2,1)S(1)}, u32[]{:S(2)}, u32[]{:S(2)}) collective-permute-start(bf16[16,6,80]{2,1,0:T(8,128)(2,1)S(1)} %reshape.337), channel_id=1, source_target_pairs={{1,0},{2,1},{3,2},{4,3},{5,4},{6,5},{7,6},{8,7},{9,8},{10,9},{11,1... | collective-permute-start | bytes 46088 | tf_op jit(solution)/shard_map/ppermute | solution.py:25
  45.5 8.7 %collective-permute-start.2 = (bf16[16,6,80]{2,1,0:T(8,128)(2,1)S(1)}, bf16[16,6,80]{2,1,0:T(8,128)(2,1)S(1)}, u32[]{:S(2)}, u32[]{:S(2)}) collective-permute-start(bf16[16,6,80]{2,1,0:T(8,128)(2,1)S(1)} %reshape.337), channel_id=1, source_target_pairs={{511,0},{0,1},{1,2},{2,3},{3,4},{4,5},{5,6},{6,7},{7,8},{8,9},{9,1... | collective-permute-start | bytes 46088 | tf_op jit(solution)/shard_map/ppermute | solution.py:25
  59.7 10.2 %collective-permute-start.5 = (bf16[16,6,80]{2,1,0:T(8,128)(2,1)S(1)}, bf16[16,6,80]{2,1,0:T(8,128)(2,1)S(1)}, u32[]{:S(2)}, u32[]{:S(2)}) collective-permute-start(bf16[16,6,80]{2,1,0:T(8,128)(2,1)S(1)} %reshape.341), channel_id=1, source_target_pairs={{1,0},{2,1},{3,2},{4,3},{5,4},{6,5},{7,6},{8,7},{9,8},{10,9},{11,1... | collective-permute-start | bytes 46088 | tf_op jit(solution)/shard_map/ppermute | solution.py:25
  67.9 5.8 %collective-permute-start.4 = (bf16[16,6,80]{2,1,0:T(8,128)(2,1)S(1)}, bf16[16,6,80]{2,1,0:T(8,128)(2,1)S(1)}, u32[]{:S(2)}, u32[]{:S(2)}) collective-permute-start(bf16[16,6,80]{2,1,0:T(8,128)(2,1)S(1)} %reshape.341), channel_id=1, source_target_pairs={{511,0},{0,1},{1,2},{2,3},{3,4},{4,5},{5,6},{6,7},{7,8},{8,9},{9,1... | collective-permute-start | bytes 46088 | tf_op jit(solution)/shard_map/ppermute | solution.py:25
  75.7 8.5 %collective-permute-start.6 = (f32[8,320]{1,0:T(8,128)S(1)}, f32[8,320]{1,0:T(8,128)S(1)}, u32[]{:S(2)}, u32[]{:S(2)}) collective-permute-start(f32[8,320]{1,0:T(8,128)S(1)} %fusion.145), channel_id=1, source_target_pairs={{0,1},{1,0},{2,3},{3,2},{4,5},{5,4},{6,7},{7,6},{8,9},{9,8},{10,11... | collective-permute-start | bytes 30728 | tf_op jit(solution)/shard_map/ppermute | solution.py:17
  84.1 7.1 %collective-permute-start.7 = (f32[8,320]{1,0:T(8,128)S(1)}, f32[8,320]{1,0:T(8,128)S(1)}, u32[]{:S(2)}, u32[]{:S(2)}) collective-permute-start(f32[8,320]{1,0:T(8,128)S(1)} %add.601), channel_id=1, source_target_pairs={{0,2},{1,3},{2,0},{3,1},{4,6},{5,7},{6,4},{7,5},{8,10},{9,11},{10,... | collective-permute-start | bytes 30728 | tf_op jit(solution)/shard_map/ppermute | solution.py:17
  93.9 4.4 %collective-permute-start.9 = (bf16[8,6,80]{2,1,0:T(8,128)(2,1)S(1)}, bf16[8,6,80]{2,1,0:T(8,128)(2,1)S(1)}, u32[]{:S(2)}, u32[]{:S(2)}) collective-permute-start(bf16[8,6,80]{2,1,0:T(8,128)(2,1)S(1)} %reshape.345), channel_id=1, source_target_pairs={{4,0},{8,4},{12,8},{16,12},{20,16},{24,20},{28,24},{32,28},{36,32}... | collective-permute-start | bytes 23048 | tf_op jit(solution)/shard_map/ppermute | solution.py:25
  95.9 8.4 %collective-permute-start.8 = (bf16[8,6,80]{2,1,0:T(8,128)(2,1)S(1)}, bf16[8,6,80]{2,1,0:T(8,128)(2,1)S(1)}, u32[]{:S(2)}, u32[]{:S(2)}) collective-permute-start(bf16[8,6,80]{2,1,0:T(8,128)(2,1)S(1)} %reshape.345), channel_id=1, source_target_pairs={{508,0},{0,4},{4,8},{8,12},{12,16},{16,20},{20,24},{24,28},{28,32}... | collective-permute-start | bytes 23048 | tf_op jit(solution)/shard_map/ppermute | solution.py:25
  108.5 4.4 %collective-permute-start.11 = (bf16[8,6,80]{2,1,0:T(8,128)(2,1)S(1)}, bf16[8,6,80]{2,1,0:T(8,128)(2,1)S(1)}, u32[]{:S(2)}, u32[]{:S(2)}) collective-permute-start(bf16[8,6,80]{2,1,0:T(8,128)(2,1)S(1)} %reshape.349), channel_id=1, source_target_pairs={{4,0},{8,4},{12,8},{16,12},{20,16},{24,20},{28,24},{32,28},{36,32}... | collective-permute-start | bytes 23048 | tf_op jit(solution)/shard_map/ppermute | solution.py:25
  110.4 8.4 %collective-permute-start.10 = (bf16[8,6,80]{2,1,0:T(8,128)(2,1)S(1)}, bf16[8,6,80]{2,1,0:T(8,128)(2,1)S(1)}, u32[]{:S(2)}, u32[]{:S(2)}) collective-permute-start(bf16[8,6,80]{2,1,0:T(8,128)(2,1)S(1)} %reshape.349), channel_id=1, source_target_pairs={{508,0},{0,4},{4,8},{8,12},{12,16},{16,20},{20,24},{24,28},{28,32}... | collective-permute-start | bytes 23048 | tf_op jit(solution)/shard_map/ppermute | solution.py:25
  122.2 5.9 %collective-permute-start.13 = (bf16[16,6,80]{2,1,0:T(8,128)(2,1)S(1)}, bf16[16,6,80]{2,1,0:T(8,128)(2,1)S(1)}, u32[]{:S(2)}, u32[]{:S(2)}) collective-permute-start(bf16[16,6,80]{2,1,0:T(8,128)(2,1)S(1)} %reshape.353), channel_id=1, source_target_pairs={{1,0},{2,1},{3,2},{4,3},{5,4},{6,5},{7,6},{8,7},{9,8},{10,9},{11,1... | collective-permute-start | bytes 46088 | tf_op jit(solution)/shard_map/ppermute | solution.py:25
  126.1 5.8 %collective-permute-start.12 = (bf16[16,6,80]{2,1,0:T(8,128)(2,1)S(1)}, bf16[16,6,80]{2,1,0:T(8,128)(2,1)S(1)}, u32[]{:S(2)}, u32[]{:S(2)}) collective-permute-start(bf16[16,6,80]{2,1,0:T(8,128)(2,1)S(1)} %reshape.353), channel_id=1, source_target_pairs={{511,0},{0,1},{1,2},{2,3},{3,4},{4,5},{5,6},{6,7},{7,8},{8,9},{9,1... | collective-permute-start | bytes 46088 | tf_op jit(solution)/shard_map/ppermute | solution.py:25
  137.3 8.7 %collective-permute-start.15 = (bf16[16,6,80]{2,1,0:T(8,128)(2,1)S(1)}, bf16[16,6,80]{2,1,0:T(8,128)(2,1)S(1)}, u32[]{:S(2)}, u32[]{:S(2)}) collective-permute-start(bf16[16,6,80]{2,1,0:T(8,128)(2,1)S(1)} %reshape.357), channel_id=1, source_target_pairs={{1,0},{2,1},{3,2},{4,3},{5,4},{6,5},{7,6},{8,7},{9,8},{10,9},{11,1... | collective-permute-start | bytes 46088 | tf_op jit(solution)/shard_map/ppermute | solution.py:25
  144.1 5.8 %collective-permute-start.14 = (bf16[16,6,80]{2,1,0:T(8,128)(2,1)S(1)}, bf16[16,6,80]{2,1,0:T(8,128)(2,1)S(1)}, u32[]{:S(2)}, u32[]{:S(2)}) collective-permute-start(bf16[16,6,80]{2,1,0:T(8,128)(2,1)S(1)} %reshape.357), channel_id=1, source_target_pairs={{511,0},{0,1},{1,2},{2,3},{3,4},{4,5},{5,6},{6,7},{7,8},{8,9},{9,1... | collective-permute-start | bytes 46088 | tf_op jit(solution)/shard_map/ppermute | solution.py:25
  155.4 8.9 %collective-permute-start.17 = (bf16[16,6,80]{2,1,0:T(8,128)(2,1)S(1)}, bf16[16,6,80]{2,1,0:T(8,128)(2,1)S(1)}, u32[]{:S(2)}, u32[]{:S(2)}) collective-permute-start(bf16[16,6,80]{2,1,0:T(8,128)(2,1)S(1)} %reshape.361), channel_id=1, source_target_pairs={{1,0},{2,1},{3,2},{4,3},{5,4},{6,5},{7,6},{8,7},{9,8},{10,9},{11,1... | collective-permute-start | bytes 46088 | tf_op jit(solution)/shard_map/ppermute | solution.py:25
  162.2 5.8 %collective-permute-start.16 = (bf16[16,6,80]{2,1,0:T(8,128)(2,1)S(1)}, bf16[16,6,80]{2,1,0:T(8,128)(2,1)S(1)}, u32[]{:S(2)}, u32[]{:S(2)}) collective-permute-start(bf16[16,6,80]{2,1,0:T(8,128)(2,1)S(1)} %reshape.361), channel_id=1, source_target_pairs={{511,0},{0,1},{1,2},{2,3},{3,4},{4,5},{5,6},{6,7},{7,8},{8,9},{9,1... | collective-permute-start | bytes 46088 | tf_op jit(solution)/shard_map/ppermute | solution.py:25
  173.4 8.7 %collective-permute-start.19 = (bf16[16,6,80]{2,1,0:T(8,128)(2,1)S(1)}, bf16[16,6,80]{2,1,0:T(8,128)(2,1)S(1)}, u32[]{:S(2)}, u32[]{:S(2)}) collective-permute-start(bf16[16,6,80]{2,1,0:T(8,128)(2,1)S(1)} %reshape.365), channel_id=1, source_target_pairs={{1,0},{2,1},{3,2},{4,3},{5,4},{6,5},{7,6},{8,7},{9,8},{10,9},{11,1... | collective-permute-start | bytes 46088 | tf_op jit(solution)/shard_map/ppermute | solution.py:25
  180.2 5.8 %collective-permute-start.18 = (bf16[16,6,80]{2,1,0:T(8,128)(2,1)S(1)}, bf16[16,6,80]{2,1,0:T(8,128)(2,1)S(1)}, u32[]{:S(2)}, u32[]{:S(2)}) collective-permute-start(bf16[16,6,80]{2,1,0:T(8,128)(2,1)S(1)} %reshape.365), channel_id=1, source_target_pairs={{511,0},{0,1},{1,2},{2,3},{3,4},{4,5},{5,6},{6,7},{7,8},{8,9},{9,1... | collective-permute-start | bytes 46088 | tf_op jit(solution)/shard_map/ppermute | solution.py:25
  188.0 8.4 %collective-permute-start.20 = (f32[8,320]{1,0:T(8,128)S(1)}, f32[8,320]{1,0:T(8,128)S(1)}, u32[]{:S(2)}, u32[]{:S(2)}) collective-permute-start(f32[8,320]{1,0:T(8,128)S(1)} %fusion.144), channel_id=1, source_target_pairs={{0,1},{1,0},{2,3},{3,2},{4,5},{5,4},{6,7},{7,6},{8,9},{9,8},{10,11... | collective-permute-start | bytes 30728 | tf_op jit(solution)/shard_map/ppermute | solution.py:17
  196.5 7.1 %collective-permute-start.21 = (f32[8,320]{1,0:T(8,128)S(1)}, f32[8,320]{1,0:T(8,128)S(1)}, u32[]{:S(2)}, u32[]{:S(2)}) collective-permute-start(f32[8,320]{1,0:T(8,128)S(1)} %add.620), channel_id=1, source_target_pairs={{0,2},{1,3},{2,0},{3,1},{4,6},{5,7},{6,4},{7,5},{8,10},{9,11},{10,... | collective-permute-start | bytes 30728 | tf_op jit(solution)/shard_map/ppermute | solution.py:17
  204.6 4.3 %collective-permute-start.23 = (bf16[8,6,80]{2,1,0:T(8,128)(2,1)S(1)}, bf16[8,6,80]{2,1,0:T(8,128)(2,1)S(1)}, u32[]{:S(2)}, u32[]{:S(2)}) collective-permute-start(bf16[8,6,80]{2,1,0:T(8,128)(2,1)S(1)} %reshape.369), channel_id=1, source_target_pairs={{4,0},{8,4},{12,8},{16,12},{20,16},{24,20},{28,24},{32,28},{36,32}... | collective-permute-start | bytes 23048 | tf_op jit(solution)/shard_map/ppermute | solution.py:25
  206.5 8.4 %collective-permute-start.22 = (bf16[8,6,80]{2,1,0:T(8,128)(2,1)S(1)}, bf16[8,6,80]{2,1,0:T(8,128)(2,1)S(1)}, u32[]{:S(2)}, u32[]{:S(2)}) collective-permute-start(bf16[8,6,80]{2,1,0:T(8,128)(2,1)S(1)} %reshape.369), channel_id=1, source_target_pairs={{508,0},{0,4},{4,8},{8,12},{12,16},{16,20},{20,24},{24,28},{28,32}... | collective-permute-start | bytes 23048 | tf_op jit(solution)/shard_map/ppermute | solution.py:25
  217.6 4.3 %collective-permute-start.25 = (bf16[8,6,80]{2,1,0:T(8,128)(2,1)S(1)}, bf16[8,6,80]{2,1,0:T(8,128)(2,1)S(1)}, u32[]{:S(2)}, u32[]{:S(2)}) collective-permute-start(bf16[8,6,80]{2,1,0:T(8,128)(2,1)S(1)} %reshape.373), channel_id=1, source_target_pairs={{4,0},{8,4},{12,8},{16,12},{20,16},{24,20},{28,24},{32,28},{36,32}... | collective-permute-start | bytes 23048 | tf_op jit(solution)/shard_map/ppermute | solution.py:25
  219.6 8.4 %collective-permute-start.24 = (bf16[8,6,80]{2,1,0:T(8,128)(2,1)S(1)}, bf16[8,6,80]{2,1,0:T(8,128)(2,1)S(1)}, u32[]{:S(2)}, u32[]{:S(2)}) collective-permute-start(bf16[8,6,80]{2,1,0:T(8,128)(2,1)S(1)} %reshape.373), channel_id=1, source_target_pairs={{508,0},{0,4},{4,8},{8,12},{12,16},{16,20},{20,24},{24,28},{28,32}... | collective-permute-start | bytes 23048 | tf_op jit(solution)/shard_map/ppermute | solution.py:25
  (4 other events, 72.8 us)
Sparse Core Ops, SparseCore 0:
  21.1 38.3 all-gather.2
